TPU v7x, 32 devices: a whole 2x2x4 slice. The times are simulated.
32 devices in a mesh: groups: 2 (over y), tile: 4 (over z), col: 2 (over x), branch: 2 (over core).
Axes of the slice: x: 2, y: 2, z: 4, core: 2. Of those that a mesh axis runs over, the one named last changes fastest.
Arguments:
- alignment_tensor: float32 [4, 64, 256, 256], P(('groups', 'branch'), 'tile', 'col'), parts along dimension 0, may hold values from -6 to 6
- residue_grid: float32 [4, 256, 256, 128], P(('groups', 'branch'), 'tile', 'col'), parts along dimension 0, may hold values from -6 to 6
- mixing_scale_vector: float32 [256], replicated, may hold values from 0.1 to 1.9
- logit_offset_scale: float32 [128], replicated, may hold values from 0.1 to 1.9
- feedforward_scale: float32 [256], replicated, may hold values from 0.1 to 1.9
- product_scale_vector: float32 [256], replicated, may hold values from 0.1 to 1.9
- grid_scale_vector: float32 [128], replicated, may hold values from 0.1 to 1.9
- logit_offset_map: float32 [128, 8], replicated, may hold values from -0.5 to 0.5
- asking_mapping: bfloat16 [256, 256], replicated, may hold values from -0.375 to 0.375
- lookup_mapping: bfloat16 [256, 256], replicated, may hold values from -0.375 to 0.375
- content_mapping: bfloat16 [256, 256], replicated, may hold values from -0.375 to 0.375
- mixing_return_matrix: bfloat16 [256, 256], replicated, may hold values from -0.375 to 0.375
- alignment_widen_map: bfloat16 [256, 1024], replicated, may hold values from -0.375 to 0.375
- alignment_shrink_map: bfloat16 [1024, 256], replicated, may hold values from -0.1875 to 0.1875
- former_embedding_map: bfloat16 [256, 32], replicated, may hold values from -0.375 to 0.375
- latter_embedding_map: bfloat16 [256, 32], replicated, may hold values from -0.375 to 0.375
- product_return_map: float32 [1024, 128], replicated, may hold values from -1 to 1
- grid_widen_map: bfloat16 [128, 512], replicated, may hold values from -0.5 to 0.5
- grid_shrink_map: bfloat16 [512, 128], replicated, may hold values from -0.25 to 0.25
Outputs:
- alignment_revised: float32 [4, 64, 256, 256], P(('groups', 'branch'), 'tile', 'col'), parts along dimension 0
- grid_revised: float32 [4, 256, 256, 128], P(('groups', 'branch'), 'tile', 'col'), parts along dimension 0
There are 2 independent parts, one for each index of `groups`. A program takes and returns all parts, laid end to end along the dimension named above; an argument that names none is the same for every part. Nothing has to cross between parts.
All inputs are finite; a program needn't handle non-finite values.
Results may differ from a plain program's by a relative error of at most 0.0075.
Values may be sent and summed in bfloat16 or wider, within the bound.
No kernel may reach another device: no remote copies, remote signals or barrier semaphores. Data moves between devices by JAX's collectives and lax.ppermute only.
A program may use at most 128 MiB of HBM per device.

v0:
```python
import jax
import jax.numpy as jnp
from jax import lax
from jax.sharding import PartitionSpec as P

SEQUENCE_DEPTH = 64


def standardize_features(x, gain):
    mean = jnp.mean(x, axis=-1, keepdims=True)
    var = jnp.mean((x - mean) ** 2, axis=-1, keepdims=True)
    return (x - mean) * lax.rsqrt(var + 1e-05) * gain


def on_device(
    alignment_tensor,
    residue_grid,
    mixing_scale_vector,
    logit_offset_scale,
    feedforward_scale,
    product_scale_vector,
    grid_scale_vector,
    logit_offset_map,
    asking_mapping,
    lookup_mapping,
    content_mapping,
    mixing_return_matrix,
    alignment_widen_map,
    alignment_shrink_map,
    former_embedding_map,
    latter_embedding_map,
    product_return_map,
    grid_widen_map,
    grid_shrink_map,
):
    sample_alignment = alignment_tensor[0]
    local_pair = residue_grid[0]
    subspace_total = logit_offset_map.shape[1]
    feature_extent = sample_alignment.shape[-1]
    subspace_number = feature_extent // subspace_total
    sequences_available = sample_alignment.shape[0]
    chain_available = sample_alignment.shape[1]
    tile_rows = local_pair.shape[0]
    tile_cols = local_pair.shape[1]
    product_extent = former_embedding_map.shape[1]
    product_operands = standardize_features(sample_alignment, product_scale_vector).astype(
        jnp.bfloat16
    )
    former_tensor = jnp.dot(
        product_operands, former_embedding_map, preferred_element_type=jnp.float32
    ).astype(jnp.bfloat16)
    latter_tensor = jnp.dot(
        product_operands, latter_embedding_map, preferred_element_type=jnp.float32
    ).astype(jnp.bfloat16)
    left_rows, right_rows = (
        lax.all_gather(former_tensor, "tile", axis=0, tiled=True),
        lax.all_gather(latter_tensor, "tile", axis=0, tiled=True),
    )
    left_all = lax.all_gather(left_rows, "col", axis=1, tiled=True)
    left_mine = lax.dynamic_slice_in_dim(left_all, lax.axis_index("tile") * tile_rows, tile_rows, 1)
    tensor_product = (
        jnp.einsum("era,eyq->ryaq", left_mine, right_rows, preferred_element_type=jnp.float32)
        / SEQUENCE_DEPTH
    )
    update = jnp.dot(
        tensor_product.reshape(tile_rows, tile_cols, product_extent * product_extent),
        product_return_map,
        precision=lax.Precision.HIGHEST,
    )
    bias_tile = jnp.einsum(
        "ijc,ch->hij",
        standardize_features(local_pair, logit_offset_scale),
        logit_offset_map,
        precision=lax.Precision.HIGHEST,
    )
    wide = lax.all_gather(bias_tile, "col", axis=2, tiled=True)
    whole = lax.all_gather(wide.astype(jnp.bfloat16), "tile", axis=1, tiled=True).astype(wide.dtype)
    bias = lax.dynamic_slice_in_dim(
        whole, lax.axis_index("col") * chain_available, chain_available, 1
    )
    standardized_source = standardize_features(sample_alignment, mixing_scale_vector).astype(
        jnp.bfloat16
    )
    asking_vectors = jnp.dot(
        standardized_source, asking_mapping, preferred_element_type=jnp.float32
    ).astype(jnp.bfloat16)
    lookup_vectors = jnp.dot(
        standardized_source, lookup_mapping, preferred_element_type=jnp.float32
    ).astype(jnp.bfloat16)
    content_vectors = jnp.dot(
        standardized_source, content_mapping, preferred_element_type=jnp.float32
    ).astype(jnp.bfloat16)
    all_keys, all_values = (
        lax.all_gather(lookup_vectors, "col", axis=1, tiled=True),
        lax.all_gather(content_vectors, "col", axis=1, tiled=True),
    )
    total_res = all_keys.shape[1]
    asking_vectors = asking_vectors.reshape(
        sequences_available, chain_available, subspace_total, subspace_number
    )
    all_keys = all_keys.reshape(sequences_available, total_res, subspace_total, subspace_number)
    all_values = all_values.reshape(sequences_available, total_res, subspace_total, subspace_number)
    scores = (
        jnp.einsum("sqhd,skhd->shqk", asking_vectors, all_keys, preferred_element_type=jnp.float32)
        / jnp.sqrt(jnp.float32(subspace_number))
        + bias[None]
    )
    weights = jax.nn.softmax(scores, axis=-1).astype(jnp.bfloat16)
    mixing_outcome = jnp.einsum(
        "shqk,skhd->sqhd", weights, all_values, preferred_element_type=jnp.float32
    )
    mixing_outcome = mixing_outcome.astype(jnp.bfloat16).reshape(
        sequences_available, chain_available, feature_extent
    )
    alignment_activations = sample_alignment + jnp.dot(
        mixing_outcome, mixing_return_matrix, preferred_element_type=jnp.float32
    )
    expanded_features = jax.nn.relu(
        jnp.dot(
            standardize_features(alignment_activations, feedforward_scale).astype(jnp.bfloat16),
            alignment_widen_map,
            preferred_element_type=jnp.float32,
        )
    ).astype(jnp.bfloat16)
    alignment_revised = alignment_activations + jnp.dot(
        expanded_features, alignment_shrink_map, preferred_element_type=jnp.float32
    )
    pair_mid = local_pair + update
    spread = jax.nn.relu(
        jnp.dot(
            standardize_features(pair_mid, grid_scale_vector).astype(jnp.bfloat16),
            grid_widen_map,
            preferred_element_type=jnp.float32,
        )
    ).astype(jnp.bfloat16)
    grid_revised = pair_mid + jnp.dot(spread, grid_shrink_map, preferred_element_type=jnp.float32)
    return (alignment_revised[None], grid_revised[None])


def solution(mesh):
    placed = (
        P(("groups", "branch"), "tile", "col", None),
        P(("groups", "branch"), "tile", "col", None),
        P(),
        P(),
        P(),
        P(),
        P(),
        P(),
        P(),
        P(),
        P(),
        P(),
        P(),
        P(),
        P(),
        P(),
        P(),
        P(),
        P(),
    )
    return jax.shard_map(
        on_device,
        mesh=mesh,
        in_specs=placed,
        out_specs=(
            P(("groups", "branch"), "tile", "col", None),
            P(("groups", "branch"), "tile", "col", None),
        ),
        check_vma=False,
    )
```

profile of v0, /device:TPU:0, one launch (start us, length us, event | category | flops | bytes accessed | tf_op | source)
XLA Modules:
  0.0 222.1 jit_solution(14404370128680419553)
XLA Ops:
  7.2 0.0 copy-start
  7.2 0.0 copy-start.2
  7.2 0.0 all-gather.11.cloned.1.call-start
  7.3 2.1 reduce_sum.89
  9.4 2.2 %multiply_reduce_fusion.3 = f32[16,128]{1,0:T(8,128)S(1)} fusion(f32[1,16,128,256]{3,2,1,0:T(8,128)} %param.19, f32[16,128]{1,0:T(8,128)S(1)} %broadcast_multiply_fusion.3), kind=kLoop, calls=%fused_computation.38 | loop fusion | flops 1570816 | bytes 2113536 | tf_op jit(solution)/shard_map/reduce_sum | solution.py:11
  11.6 0.9 convolution_convert_fusion.3
  12.6 17.4 %all_gather.26 = bf16[64,128,32]{1,2,0:T(8,128)(2,1)S(1)} all-gather(bf16[16,128,32]{1,2,0:T(8,128)(2,1)S(1)} %convolution_convert_fusion.3), channel_id=1, replica_groups=mesh['groups'=2,'tile'=4,'col'=2,'branch'=2] {'tile'}, dimensions={0}, use_global_device_ids=true | all-gather | bytes 655360 | tf_op jit(solution)/shard_map/all_gather | solution.py:56
  30.0 1.6 copy.65
  31.6 0.0 all-gather.11.cloned.1.call-update
  31.6 0.0 all-gather.9.cloned.1.call-start
  31.7 5.6 %copy.61 = f32[1,64,128,128]{2,3,1,0:T(8,128)} copy(f32[1,64,128,128]{3,2,1,0:T(8,128)} %param.20) | data formatting | bytes 8388608 | tf_op args[1]
  37.3 3.4 %reduce_sum.91 = f32[64,128]{1,0:T(8,128)S(1)} reduce(f32[1,64,128,128]{3,2,1,0:T(8,128)} %param.20, f32[]{:T(128)} %constant.17.clone.1), dimensions={0,3}, to_apply=%region_2.0 | reduce | flops 1040384 | bytes 4227076 | tf_op jit(solution)/shard_map/reduce_sum | solution.py:10
  40.7 0.0 copy-start.16
  40.7 3.5 %multiply_reduce_fusion.1 = f32[64,128]{1,0:T(8,128)S(1)} fusion(f32[1,64,128,128]{2,3,1,0:T(8,128)} %copy.61, f32[64,128]{1,0:T(8,128)S(1)} %broadcast_multiply_fusion.1), kind=kLoop, calls=%fused_computation.21 | loop fusion | flops 3137536 | bytes 4259840 | tf_op jit(solution)/shard_map/reduce_sum | solution.py:11
  44.3 0.4 copy-done.3
  44.6 2.7 %fusion.26 = bf16[8,64,128]{2,0,1:T(8,128)(2,1)S(1)} fusion(f32[1,64,128,128]{2,3,1,0:T(8,128)S(1)} %copy-done.3, f32[128]{0:T(128)S(1)} %copy-done.18, f32[64,128]{1,0:T(8,128)S(1)} %add_rsqrt_fusion.1, f32[64,128]{1,0:T(8,128)S(1)} %broadcast_multiply_fusion.1, f32[128,8]{0,1:T(8,128)S(1)} %copy-done.15), kind=kOutput, calls=%fused_computation.44 | convolution fusion | flops 103809024 | bytes 4395520 | tf_op jit(solution)/shard_map/ijc,ch->hij/dot_general | solution.py:70
  47.3 9.4 %all_gather.23 = bf16[8,64,256]{2,0,1:T(8,128)(2,1)} all-gather(bf16[8,64,128]{2,0,1:T(8,128)(2,1)S(1)} %fusion.26), channel_id=1, replica_groups=mesh['groups'=2,'tile'=4,'col'=2,'branch'=2] {'col'}, dimensions={2}, use_global_device_ids=true | all-gather | bytes 393216 | tf_op jit(solution)/shard_map/all_gather | solution.py:76
  56.7 0.0 all-gather.9.cloned.1.call-update
  56.8 0.0 all-gather.7.cloned.1.call-start
  56.8 0.7 multiply_convert_fusion.5
  57.5 0.0 copy-start.4
  57.6 1.0 copy-done.4
  58.5 1.5 convolution_convert_fusion
  60.0 0.0 all-gather.7.cloned.1.call-update
  60.0 0.0 all-gather.5.cloned.1.call-start
  60.1 2.6 %convolution_convert_fusion.2 = bf16[16,128,256]{2,1,0:T(8,128)(2,1)} fusion(bf16[16,128,256]{2,1,0:T(8,128)(2,1)} %copy-done.4, bf16[256,256]{1,0:T(8,128)(2,1)S(1)} %copy-done.9), kind=kOutput, calls=%fused_computation.43 | convolution fusion | flops 268959744 | bytes 2228224 | tf_op jit(solution)/shard_map/dot_general | solution.py:90
  62.7 0.0 all-gather.5.cloned.1.call-update
  62.8 0.9 convolution_convert_fusion.4
  63.7 16.1 %all_gather.25 = bf16[64,128,32]{1,2,0:T(8,128)(2,1)S(1)} all-gather(bf16[16,128,32]{1,2,0:T(8,128)(2,1)S(1)} %convolution_convert_fusion.4), channel_id=1, replica_groups=mesh['groups'=2,'tile'=4,'col'=2,'branch'=2] {'tile'}, dimensions={0}, use_global_device_ids=true | all-gather | bytes 655360 | tf_op jit(solution)/shard_map/all_gather | solution.py:57
  79.8 2.7 %convolution_convert_fusion.1 = bf16[16,128,256]{2,1,0:T(8,128)(2,1)} fusion(bf16[16,128,256]{2,1,0:T(8,128)(2,1)} %copy-done.4, bf16[256,256]{1,0:T(8,128)(2,1)S(1)} %copy-done.10), kind=kOutput, calls=%fused_computation.42 | convolution fusion | flops 268959744 | bytes 2228224 | tf_op jit(solution)/shard_map/dot_general | solution.py:84
  82.5 2.3 %copy.59 = bf16[16,128,256]{1,2,0:T(8,128)(2,1)} copy(bf16[16,128,256]{2,1,0:T(8,128)(2,1)} %convolution_convert_fusion.1) | data formatting | bytes 2097152 | tf_op jit(solution)/shard_map/convert_element_type | solution.py:86
  84.8 14.2 %multiply_bitcast_fusion = f32[64,128,32,32]{1,0,2,3:T(8,128)} fusion(bf16[64,128,32,1]{1,2,0,3:T(8,128)(2,1)S(1)} %bitcast.95, bf16[64,256,32]{0,1,2:T(8,128)(2,1)} %all-gather.11.cloned.1.call-done, s32[]{:T(128)S(6)} %select_n.7), kind=kOutput, calls=%fused_computation.1 | convolution fusion | flops 1082130432 | bytes 34603012 | tf_op jit(solution)/shard_map/era,eyq->ryaq/dot_general | solution.py:62
  99.1 32.0 %copy.67 = f32[64,128,32,32]{1,3,2,0:T(8,128)} copy(f32[64,128,32,32]{1,0,2,3:T(8,128)} %multiply_bitcast_fusion) | data formatting | bytes 67108864 | tf_op jit(solution)/shard_map/div | solution.py:62
  131.0 25.6 %fusion.58 = (f32[64,128]{1,0:T(8,128)S(1)}, f32[64,128,128]{1,2,0:T(8,128)}) fusion(f32[64,128,1024]{1,2,0:T(8,128)} %bitcast.94, f32[1024,128]{1,0:T(8,128)S(1)} %copy-done, f32[1,64,128,128]{2,3,1,0:T(8,128)} %copy.61), kind=kOutput, calls=%fused_computation.80 | convolution fusion | flops 12886990848 | bytes 42500096 | tf_op jit(solution)/shard_map/dot_general | solution.py:65
  156.7 3.0 %multiply_reduce_fusion = f32[64,128]{1,0:T(8,128)S(1)} fusion(f32[64,128,128]{1,2,0:T(8,128)} %get-tuple-element.15, f32[64,128]{1,0:T(8,128)S(1)} %broadcast_multiply_fusion), kind=kLoop, calls=%fused_computation.16 | loop fusion | flops 3137536 | bytes 4259840 | tf_op jit(solution)/shard_map/reduce_sum | solution.py:11
  159.8 10.1 %add_bitcast_fusion = f32[1,64,128,128]{2,3,1,0:T(8,128)} fusion(f32[64,128,128]{1,2,0:T(8,128)} %get-tuple-element.15, f32[128]{0:T(128)S(1)} %copy-done.17, f32[64,128]{1,0:T(8,128)S(1)} %add_rsqrt_fusion, f32[64,128]{1,0:T(8,128)S(1)} %broadcast_multiply_fusion, bf16[512,128]{1,0:T(8,128)(2,1)S(1)} %copy-done.6, bf16[128,512]{1,0:T(8,128)(2,1)S(1)} %copy-done.7), kind=kOutput, calls=%fused_computation.14 | convolution fusion | flops 2161115136 | bytes 8716800 | tf_op jit(solution)/shard_map/dot_general | solution.py:136
  169.9 5.6 %copy.72 = f32[1,64,128,128]{3,2,1,0:T(8,128)} copy(f32[1,64,128,128]{2,3,1,0:T(8,128)} %add_bitcast_fusion) | data formatting | bytes 8388608
  175.5 1.1 dynamic-slice_convert_fusion
  176.6 1.3 copy.63
  177.9 3.9 %copy.60 = bf16[16,256,256]{1,2,0:T(8,128)(2,1)} copy(bf16[16,256,256]{2,1,0:T(8,128)(2,1)} %all-gather.7.cloned.1.call-done) | data formatting | bytes 4194304 | tf_op jit(solution)/shard_map/all_gather | solution.py:94
  181.8 12.4 %fusion.56 = (f32[16,8,128]{2,1,0:T(8,128)S(1)}, f32[16,8,128,256]{3,2,1,0:T(8,128)}) fusion(f32[8,128,256]{2,1,0:T(8,128)} %copy.63, bf16[16,128,8,32]{1,3,2,0:T(8,128)(2,1)} %bitcast.98, bf16[16,256,8,32]{1,3,2,0:T(8,128)(2,1)} %bitcast.96), kind=kOutput, calls=%fused_computation.78 | convolution fusion | flops 285212928 | bytes 21037056 | tf_op jit(solution)/shard_map/sub | solution.py:108
  194.2 3.9 %copy.58 = bf16[16,256,256]{1,2,0:T(8,128)(2,1)} copy(bf16[16,256,256]{2,1,0:T(8,128)(2,1)} %all-gather.5.cloned.1.call-done) | data formatting | bytes 4194304 | tf_op jit(solution)/shard_map/all_gather | solution.py:95
  198.1 8.3 %fusion.25 = bf16[16,8,32,128]{3,2,1,0:T(8,128)(2,1)S(1)} fusion(bf16[16,256,8,32]{1,3,2,0:T(8,128)(2,1)} %bitcast.97, f32[16,8,128,256]{3,2,1,0:T(8,128)} %get-tuple-element.11, f32[16,8,128]{2,1,0:T(8,128)S(1)} %get-tuple-element.10), kind=kOutput, calls=%fused_computation.40 | convolution fusion | flops 277348352 | bytes 19988480 | tf_op jit(solution)/shard_map/shqk,skhd->sqhd/dot_general | solution.py:109
  206.5 0.8 fusion.57
  207.3 1.3 copy-done.5
  208.6 0.6 multiply_reduce_fusion.2
  209.3 0.0 copy-start.1
  209.3 6.3 %add_bitcast_fusion.1 = f32[1,16,128,256]{3,2,1,0:T(8,128)} fusion(f32[16,128,256]{2,1,0:T(8,128)} %copy-done.5, f32[256]{0:T(256)S(1)} %copy-done.20, f32[16,128]{1,0:T(8,128)S(1)} %add_rsqrt_fusion.2, f32[16,128]{1,0:T(8,128)S(1)} %broadcast_multiply_fusion.2, bf16[1024,256]{1,0:T(8,128)(2,1)S(1)} %copy-done.19, bf16[256,1024]{1,0:T(8,128)(2,1)} %param.31), kind=kOutput, calls=%fused_computation.31 | convolution fusion | flops 2154299392 | bytes 5260288 | tf_op jit(solution)/shard_map/dot_general | solution.py:125
  (46 shorter events, 0.1 us)
Async XLA Ops:
  7.2 123.9 %copy-start = (f32[1024,128]{1,0:T(8,128)S(1)}, f32[1024,128]{1,0:T(8,128)}, u32[]{:S(2)}) copy-start(f32[1024,128]{1,0:T(8,128)} %param.35) | copy-start | bytes 1572868
  7.2 4.4 %copy-start.2 = (f32[1,16,128,256]{3,2,1,0:T(8,128)S(1)}, f32[1,16,128,256]{3,2,1,0:T(8,128)}, u32[]{:S(2)}) copy-start(f32[1,16,128,256]{3,2,1,0:T(8,128)} %param.19) | copy-start | bytes 6291460
  7.2 4.4 %copy-start.14 = (f32[256]{0:T(256)S(1)}, f32[256]{0:T(256)}, u32[]{:S(2)}) copy-start(f32[256]{0:T(256)} %param.24) | copy-start | bytes 3076
  7.2 4.4 %copy-start.12 = (bf16[256,32]{0,1:T(8,128)(2,1)S(1)}, bf16[256,32]{0,1:T(8,128)(2,1)}, u32[]{:S(2)}) copy-start(bf16[256,32]{0,1:T(8,128)(2,1)} %param.33) | copy-start | bytes 49156
  7.2 77.6 %all-gather.11.cloned.1.call-start = ((), (), s32[]{:S(2)}) async-start(), calls=%async_computation.3 | async-start | bytes 3145728 | tf_op jit(solution)/shard_map/all_gather | solution.py:59
  31.6 143.9 %all-gather.9.cloned.1.call-start = ((), (), s32[]{:S(2)}) async-start(), calls=%async_computation.2 | async-start | bytes 1310720 | tf_op jit(solution)/shard_map/all_gather | solution.py:77
  37.3 7.0 %copy-start.15 = (f32[128,8]{0,1:T(8,128)S(1)}, f32[128,8]{0,1:T(8,128)}, u32[]{:S(2)}) copy-start(f32[128,8]{0,1:T(8,128)} %param.26) | copy-start | bytes 12292
  37.3 7.0 %copy-start.18 = (f32[128]{0:T(128)S(1)}, f32[128]{0:T(128)}, u32[]{:S(2)}) copy-start(f32[128]{0:T(128)} %param.22) | copy-start | bytes 1540
  40.7 3.9 %copy-start.3 = (f32[1,64,128,128]{2,3,1,0:T(8,128)S(1)}, f32[1,64,128,128]{2,3,1,0:T(8,128)}, u32[]{:S(2)}) copy-start(f32[1,64,128,128]{2,3,1,0:T(8,128)} %copy.61) | copy-start | bytes 12582916
  40.7 16.1 %copy-start.16 = (f32[256]{0:T(256)S(1)}, f32[256]{0:T(256)}, u32[]{:S(2)}) copy-start(f32[256]{0:T(256)} %param.21) | copy-start | bytes 3076
  44.2 14.3 %copy-start.8 = (bf16[256,256]{1,0:T(8,128)(2,1)S(1)}, bf16[256,256]{1,0:T(8,128)(2,1)}, u32[]{:S(2)}) copy-start(bf16[256,256]{1,0:T(8,128)(2,1)} %param.28) | copy-start | bytes 393220
  47.3 12.7 %copy-start.9 = (bf16[256,256]{1,0:T(8,128)(2,1)S(1)}, bf16[256,256]{1,0:T(8,128)(2,1)}, u32[]{:S(2)}) copy-start(bf16[256,256]{1,0:T(8,128)(2,1)} %param.29) | copy-start | bytes 393220
  56.7 6.0 %copy-start.13 = (bf16[256,32]{0,1:T(8,128)(2,1)S(1)}, bf16[256,32]{0,1:T(8,128)(2,1)}, u32[]{:S(2)}) copy-start(bf16[256,32]{0,1:T(8,128)(2,1)} %param.34) | copy-start | bytes 49156
  56.8 121.2 %all-gather.7.cloned.1.call-start = ((), (), s32[]{:S(2)}) async-start(), calls=%async_computation.1 | async-start | bytes 3145728 | tf_op jit(solution)/shard_map/all_gather | solution.py:94
  57.5 1.0 copy-start.4
  60.0 19.8 %copy-start.10 = (bf16[256,256]{1,0:T(8,128)(2,1)S(1)}, bf16[256,256]{1,0:T(8,128)(2,1)}, u32[]{:S(2)}) copy-start(bf16[256,256]{1,0:T(8,128)(2,1)} %param.27) | copy-start | bytes 393220
  60.0 134.2 %all-gather.5.cloned.1.call-start = ((), (), s32[]{:S(2)}) async-start(), calls=%async_computation | async-start | bytes 3145728 | tf_op jit(solution)/shard_map/all_gather | solution.py:95
  156.7 3.1 %copy-start.6 = (bf16[512,128]{1,0:T(8,128)(2,1)S(1)}, bf16[512,128]{1,0:T(8,128)(2,1)}, u32[]{:S(2)}) copy-start(bf16[512,128]{1,0:T(8,128)(2,1)} %param.37) | copy-start | bytes 393220
  156.7 3.1 %copy-start.7 = (bf16[128,512]{1,0:T(8,128)(2,1)S(1)}, bf16[128,512]{1,0:T(8,128)(2,1)}, u32[]{:S(2)}) copy-start(bf16[128,512]{1,0:T(8,128)(2,1)} %param.36) | copy-start | bytes 393220
  156.7 3.1 %copy-start.17 = (f32[128]{0:T(128)S(1)}, f32[128]{0:T(128)}, u32[]{:S(2)}) copy-start(f32[128]{0:T(128)} %param.25) | copy-start | bytes 1540
  198.1 8.4 %copy-start.11 = (bf16[256,256]{1,0:T(8,128)(2,1)S(1)}, bf16[256,256]{1,0:T(8,128)(2,1)}, u32[]{:S(2)}) copy-start(bf16[256,256]{1,0:T(8,128)(2,1)} %param.30) | copy-start | bytes 393220
  206.4 2.8 %copy-start.19 = (bf16[1024,256]{1,0:T(8,128)(2,1)S(1)}, bf16[1024,256]{1,0:T(8,128)(2,1)}, u32[]{:S(2)}) copy-start(bf16[1024,256]{1,0:T(8,128)(2,1)} %param.32) | copy-start | bytes 1572868
  206.5 2.8 %copy-start.20 = (f32[256]{0:T(256)S(1)}, f32[256]{0:T(256)}, u32[]{:S(2)}) copy-start(f32[256]{0:T(256)} %param.23) | copy-start | bytes 3076
  207.3 1.4 copy-start.5
  209.3 6.3 %copy-start.1 = (f32[1024,128]{1,0:T(8,128)S(1)}, f32[1024,128]{1,0:T(8,128)}, u32[]{:S(2)}) copy-start(f32[1024,128]{1,0:T(8,128)} %param.35) | copy-start | bytes 1572868
Sparse Core Ops, SparseCore 0:
  31.7 37.6 all-gather.10
  71.0 27.9 all-gather.8
  100.6 32.5 all-gather.6
  134.6 33.0 all-gather.4
where the time goes:
time: 223 us; the launch traced here: 222 us
  matrix products  89.1 us (40%)
  local copies, waits for them, and re-layouts  59 us (26%)
  blocking collectives  42.9 us (19%)
  other arithmetic  16.8 us (8%)
  between operations  14.1 us (6%)
    div x1, local copies, waits for them, and re-layouts, on_device(): jnp.einsum('era,eyq->ryaq', left_mine, right_rows, preferred_element_type...  32 us
    dot_general x1, matrix products, on_device(): jnp.dot(tensor_product.reshape(tile_rows, tile_cols, product_extent * pro...  25.6 us
    all_gather x1, blocking collectives, on_device(): lax.all_gather(former_tensor, 'tile', axis=0, tiled=True)  17.4 us
    all_gather x1, blocking collectives, on_device(): lax.all_gather(latter_tensor, 'tile', axis=0, tiled=True)  16.1 us
    dot_general x1, matrix products, on_device(): jnp.einsum('era,eyq->ryaq', left_mine, right_rows, preferred_element_type...  14.2 us
    unnamed x44, local copies, waits for them, and re-layouts  14 us
    sub x1, matrix products, on_device(): weights = jax.nn.softmax(scores, axis=-1).astype(jnp.bfloat16)  12.4 us
    dot_general x1, matrix products, on_device(): jnp.dot(spread, grid_shrink_map, preferred_element_type=jnp.float32)  10.1 us
  transfers between devices with their start and end apart: 4, of which 0 were waited for; matrix products, arithmetic and copies ran while one was open for 61% of the time, Pallas kernels for 0%

commit v1 on v0

--- a/solution.py
+++ b/solution.py
@@ -53,7 +53,9 @@
         product_operands, latter_embedding_map, preferred_element_type=jnp.float32
     ).astype(jnp.bfloat16)
     left_rows, right_rows = (
-        lax.all_gather(former_tensor, "tile", axis=0, tiled=True),
+        jnp.concatenate(
+            lax.all_to_all(jnp.stack([former_tensor] * lax.axis_size("tile")), "tile", 0, 0), axis=0
+        ),
         lax.all_gather(latter_tensor, "tile", axis=0, tiled=True),
     )
     left_all = lax.all_gather(left_rows, "col", axis=1, tiled=True)

time: 223 us -> 237 us (1.063)
  blocking collectives: 42.9 us -> 53.5 us
  waiting for transfers between devices: 0.07 us -> 7.37 us
  other arithmetic: 16.8 us -> 13.1 us
    all_to_all x0 -> x1, blocking collectives: none -> 30.5 us  [on_device(): lax.all_to_all(jnp.stack([former_tensor] * lax.axis_size('tile')), 'tile'...]
    all_gather x1 -> x0, blocking collectives: 17.4 us -> none  [on_device(): lax.all_gather(former_tensor, 'tile', axis=0, tiled=True)]
    all_gather x1, waiting for transfers between devices: 0.01 us -> 7.3 us  [on_device(): left_all = lax.all_gather(left_rows, 'col', axis=1, tiled=True)]
  transfers between devices with their start and end apart: 4 -> 4, of which waited for: 0 -> 1; matrix products, arithmetic and copies ran while one was open for 61% -> 53% of each run, Pallas kernels for 0% -> 0%
where the time goes in v1:
time: 237 us
  matrix products  89.6 us (38%)
  local copies, waits for them, and re-layouts  58.7 us (25%)
  blocking collectives  53.5 us (23%)
  between operations  14.1 us (6%)
  other arithmetic  13.1 us (6%)
  waiting for transfers between devices  7.37 us (3%)
    div x1, local copies, waits for them, and re-layouts, on_device(): jnp.einsum('era,eyq->ryaq', left_mine, right_rows, preferred_element_type...  31.7 us
    all_to_all x1, blocking collectives, on_device(): lax.all_to_all(jnp.stack([former_tensor] * lax.axis_size('tile')), 'tile'...  30.5 us
    dot_general x1, matrix products, on_device(): jnp.dot(tensor_product.reshape(tile_rows, tile_cols, product_extent * pro...  25.6 us
    all_gather x1, blocking collectives, on_device(): lax.all_gather(latter_tensor, 'tile', axis=0, tiled=True)  15.7 us
    dot_general x1, matrix products, on_device(): jnp.einsum('era,eyq->ryaq', left_mine, right_rows, preferred_element_type...  15.1 us
    unnamed x44, local copies, waits for them, and re-layouts  13.8 us
    sub x1, matrix products, on_device(): weights = jax.nn.softmax(scores, axis=-1).astype(jnp.bfloat16)  12.4 us
    dot_general x1, matrix products, on_device(): jnp.dot(spread, grid_shrink_map, preferred_element_type=jnp.float32)  10.1 us
  transfers between devices with their start and end apart: 4, of which 1 were waited for; matrix products, arithmetic and copies ran while one was open for 53% of the time, Pallas kernels for 0%

profile of v1, /device:TPU:0, one launch (start us, length us, event | category | flops | bytes accessed | tf_op | source)
XLA Modules:
  0.0 236.6 jit_solution(18209784090632360822)
XLA Ops:
  7.2 0.0 copy-start
  7.2 0.0 all-gather.9.cloned.1.call-start
  7.2 5.6 %copy.63 = f32[1,64,128,128]{2,3,1,0:T(8,128)} copy(f32[1,64,128,128]{3,2,1,0:T(8,128)} %param.20) | data formatting | bytes 8388608 | tf_op args[1]
  12.9 3.4 %reduce_sum.91 = f32[64,128]{1,0:T(8,128)S(1)} reduce(f32[1,64,128,128]{3,2,1,0:T(8,128)} %param.20, f32[]{:T(128)} %constant.17.clone.1), dimensions={0,3}, to_apply=%region_2.0 | reduce | flops 1040384 | bytes 4227076 | tf_op jit(solution)/shard_map/reduce_sum | solution.py:10
  16.2 0.0 copy-start.3
  16.3 3.2 %multiply_reduce_fusion.1 = f32[64,128]{1,0:T(8,128)S(1)} fusion(f32[1,64,128,128]{2,3,1,0:T(8,128)} %copy.63, f32[64,128]{1,0:T(8,128)S(1)} %broadcast_multiply_fusion.1), kind=kLoop, calls=%fused_computation.21 | loop fusion | flops 3137536 | bytes 4259840 | tf_op jit(solution)/shard_map/reduce_sum | solution.py:11
  19.5 0.2 copy-done.3
  19.7 2.7 %fusion.26 = bf16[8,64,128]{2,0,1:T(8,128)(2,1)S(1)} fusion(f32[1,64,128,128]{2,3,1,0:T(8,128)S(1)} %copy-done.3, f32[128]{0:T(128)S(1)} %copy-done.18, f32[64,128]{1,0:T(8,128)S(1)} %add_rsqrt_fusion.1, f32[64,128]{1,0:T(8,128)S(1)} %broadcast_multiply_fusion.1, f32[128,8]{0,1:T(8,128)S(1)} %copy-done.15), kind=kOutput, calls=%fused_computation.44 | convolution fusion | flops 103809024 | bytes 4395520 | tf_op jit(solution)/shard_map/ijc,ch->hij/dot_general | solution.py:72
  22.4 7.2 %all_gather.20 = bf16[8,64,256]{2,0,1:T(8,128)(2,1)} all-gather(bf16[8,64,128]{2,0,1:T(8,128)(2,1)S(1)} %fusion.26), channel_id=1, replica_groups=mesh['groups'=2,'tile'=4,'col'=2,'branch'=2] {'col'}, dimensions={2}, use_global_device_ids=true | all-gather | bytes 393216 | tf_op jit(solution)/shard_map/all_gather | solution.py:78
  29.7 0.0 all-gather.9.cloned.1.call-update
  29.7 0.0 all-gather.11.cloned.1.call-start
  29.7 0.3 reduce_sum.89
  30.1 0.6 multiply_reduce_fusion.3
  30.8 0.9 convolution_convert_fusion.3
  31.8 0.1 stack.2
  31.8 30.5 %all_to_all.5 = bf16[4,16,128,32]{2,3,1,0:T(8,128)(2,1)S(1)} all-to-all(bf16[4,16,128,32]{2,3,1,0:T(8,128)(2,1)S(1)} %stack.2), channel_id=1, replica_groups=mesh['groups'=2,'tile'=4,'col'=2,'branch'=2] {'tile'}, dimensions={0} | all-to-all | bytes 1048576 | tf_op jit(solution)/shard_map/all_to_all | solution.py:57
  62.4 1.6 copy.67
  64.0 0.0 all-gather.11.cloned.1.call-update
  64.0 0.0 all-gather.7.cloned.1.call-start
  64.1 0.7 multiply_convert_fusion.5
  64.8 1.0 copy-done.4
  65.8 1.5 convolution_convert_fusion
  67.3 0.0 all-gather.7.cloned.1.call-update
  67.3 0.0 all-gather.5.cloned.1.call-start
  67.3 2.6 %convolution_convert_fusion.2 = bf16[16,128,256]{2,1,0:T(8,128)(2,1)} fusion(bf16[16,128,256]{2,1,0:T(8,128)(2,1)} %copy-done.4, bf16[256,256]{1,0:T(8,128)(2,1)S(1)} %copy-done.9), kind=kOutput, calls=%fused_computation.43 | convolution fusion | flops 268959744 | bytes 2228224 | tf_op jit(solution)/shard_map/dot_general | solution.py:92
  70.0 0.0 all-gather.5.cloned.1.call-update
  70.0 0.9 convolution_convert_fusion.4
  71.0 15.7 %all_gather.22 = bf16[64,128,32]{1,2,0:T(8,128)(2,1)S(1)} all-gather(bf16[16,128,32]{1,2,0:T(8,128)(2,1)S(1)} %convolution_convert_fusion.4), channel_id=1, replica_groups=mesh['groups'=2,'tile'=4,'col'=2,'branch'=2] {'tile'}, dimensions={0}, use_global_device_ids=true | all-gather | bytes 655360 | tf_op jit(solution)/shard_map/all_gather | solution.py:59
  86.7 2.6 %convolution_convert_fusion.1 = bf16[16,128,256]{2,1,0:T(8,128)(2,1)} fusion(bf16[16,128,256]{2,1,0:T(8,128)(2,1)} %copy-done.4, bf16[256,256]{1,0:T(8,128)(2,1)S(1)} %copy-done.10), kind=kOutput, calls=%fused_computation.42 | convolution fusion | flops 268959744 | bytes 2228224 | tf_op jit(solution)/shard_map/dot_general | solution.py:86
  89.3 2.3 copy.61
  91.6 1.1 dynamic-slice_convert_fusion
  92.7 1.3 copy.65
  94.1 7.3 %all-gather.11.cloned.1.call-done = bf16[64,256,32]{0,1,2:T(8,128)(2,1)} async-done(((bf16[64,128,32]{0,1,2:T(8,128)(2,1)}), bf16[64,256,32]{0,1,2:T(8,128)(2,1)}) %all-gather.11.cloned.1.call-update) | async-done | bytes 1048592 | tf_op jit(solution)/shard_map/all_gather | solution.py:61
  101.4 15.1 %multiply_bitcast_fusion = f32[64,128,32,32]{1,0,2,3:T(8,128)} fusion(bf16[64,128,32,1]{1,2,0,3:T(8,128)(2,1)S(1)} %bitcast.96, bf16[64,256,32]{0,1,2:T(8,128)(2,1)} %all-gather.11.cloned.1.call-done, s32[]{:T(128)S(6)} %select_n.7), kind=kOutput, calls=%fused_computation.1 | convolution fusion | flops 1082130432 | bytes 34603012 | tf_op jit(solution)/shard_map/era,eyq->ryaq/dot_general | solution.py:64
  116.5 31.7 %copy.69 = f32[64,128,32,32]{1,3,2,0:T(8,128)} copy(f32[64,128,32,32]{1,0,2,3:T(8,128)} %multiply_bitcast_fusion) | data formatting | bytes 67108864 | tf_op jit(solution)/shard_map/div | solution.py:64
  148.2 25.6 %fusion.58 = (f32[64,128]{1,0:T(8,128)S(1)}, f32[64,128,128]{1,2,0:T(8,128)}) fusion(f32[64,128,1024]{1,2,0:T(8,128)} %bitcast.95, f32[1024,128]{1,0:T(8,128)S(1)} %copy-done, f32[1,64,128,128]{2,3,1,0:T(8,128)} %copy.63), kind=kOutput, calls=%fused_computation.80 | convolution fusion | flops 12886990848 | bytes 42500096 | tf_op jit(solution)/shard_map/dot_general | solution.py:67
  173.8 3.0 %multiply_reduce_fusion = f32[64,128]{1,0:T(8,128)S(1)} fusion(f32[64,128,128]{1,2,0:T(8,128)} %get-tuple-element.15, f32[64,128]{1,0:T(8,128)S(1)} %broadcast_multiply_fusion), kind=kLoop, calls=%fused_computation.16 | loop fusion | flops 3137536 | bytes 4259840 | tf_op jit(solution)/shard_map/reduce_sum | solution.py:11
  176.9 10.1 %add_bitcast_fusion = f32[1,64,128,128]{2,3,1,0:T(8,128)} fusion(f32[64,128,128]{1,2,0:T(8,128)} %get-tuple-element.15, f32[128]{0:T(128)S(1)} %copy-done.17, f32[64,128]{1,0:T(8,128)S(1)} %add_rsqrt_fusion, f32[64,128]{1,0:T(8,128)S(1)} %broadcast_multiply_fusion, bf16[512,128]{1,0:T(8,128)(2,1)S(1)} %copy-done.6, bf16[128,512]{1,0:T(8,128)(2,1)S(1)} %copy-done.7), kind=kOutput, calls=%fused_computation.14 | convolution fusion | flops 2161115136 | bytes 8716800 | tf_op jit(solution)/shard_map/dot_general | solution.py:138
  187.0 5.6 %copy.74 = f32[1,64,128,128]{3,2,1,0:T(8,128)} copy(f32[1,64,128,128]{2,3,1,0:T(8,128)} %add_bitcast_fusion) | data formatting | bytes 8388608
  192.6 3.9 %copy.62 = bf16[16,256,256]{1,2,0:T(8,128)(2,1)} copy(bf16[16,256,256]{2,1,0:T(8,128)(2,1)} %all-gather.7.cloned.1.call-done) | data formatting | bytes 4194304 | tf_op jit(solution)/shard_map/all_gather | solution.py:96
  196.5 12.4 %fusion.56 = (f32[16,8,128]{2,1,0:T(8,128)S(1)}, f32[16,8,128,256]{3,2,1,0:T(8,128)}) fusion(f32[8,128,256]{2,1,0:T(8,128)} %copy.65, bf16[16,128,8,32]{1,3,2,0:T(8,128)(2,1)} %bitcast.100, bf16[16,256,8,32]{1,3,2,0:T(8,128)(2,1)} %bitcast.98), kind=kOutput, calls=%fused_computation.78 | convolution fusion | flops 285212928 | bytes 21037056 | tf_op jit(solution)/shard_map/sub | solution.py:110
  208.9 3.9 %copy.60 = bf16[16,256,256]{1,2,0:T(8,128)(2,1)} copy(bf16[16,256,256]{2,1,0:T(8,128)(2,1)} %all-gather.5.cloned.1.call-done) | data formatting | bytes 4194304 | tf_op jit(solution)/shard_map/all_gather | solution.py:97
  212.8 8.1 %fusion.25 = bf16[16,8,32,128]{3,2,1,0:T(8,128)(2,1)S(1)} fusion(bf16[16,256,8,32]{1,3,2,0:T(8,128)(2,1)} %bitcast.99, f32[16,8,128,256]{3,2,1,0:T(8,128)} %get-tuple-element.11, f32[16,8,128]{2,1,0:T(8,128)S(1)} %get-tuple-element.10), kind=kOutput, calls=%fused_computation.40 | convolution fusion | flops 277348352 | bytes 19988480 | tf_op jit(solution)/shard_map/shqk,skhd->sqhd/dot_general | solution.py:111
  220.9 0.0 copy-start.19
  220.9 0.8 fusion.57
  221.7 1.3 copy-done.5
  223.1 0.6 multiply_reduce_fusion.2
  223.8 6.3 %add_bitcast_fusion.1 = f32[1,16,128,256]{3,2,1,0:T(8,128)} fusion(f32[16,128,256]{2,1,0:T(8,128)} %copy-done.5, f32[256]{0:T(256)S(1)} %copy-done.20, f32[16,128]{1,0:T(8,128)S(1)} %add_rsqrt_fusion.2, f32[16,128]{1,0:T(8,128)S(1)} %broadcast_multiply_fusion.2, bf16[1024,256]{1,0:T(8,128)(2,1)S(1)} %copy-done.19, bf16[256,1024]{1,0:T(8,128)(2,1)} %param.31), kind=kOutput, calls=%fused_computation.31 | convolution fusion | flops 2154299392 | bytes 5260288 | tf_op jit(solution)/shard_map/dot_general | solution.py:127
  (47 shorter events, 0.1 us)
Async XLA Ops:
  7.2 141.1 %copy-start = (f32[1024,128]{1,0:T(8,128)S(1)}, f32[1024,128]{1,0:T(8,128)}, u32[]{:S(2)}) copy-start(f32[1024,128]{1,0:T(8,128)} %param.35) | copy-start | bytes 1572868
  7.2 84.4 %all-gather.9.cloned.1.call-start = ((), (), s32[]{:S(2)}) async-start(), calls=%async_computation.3 | async-start | bytes 1310720 | tf_op jit(solution)/shard_map/all_gather | solution.py:79
  12.9 6.6 %copy-start.15 = (f32[128,8]{0,1:T(8,128)S(1)}, f32[128,8]{0,1:T(8,128)}, u32[]{:S(2)}) copy-start(f32[128,8]{0,1:T(8,128)} %param.26) | copy-start | bytes 12292
  12.9 6.6 %copy-start.18 = (f32[128]{0:T(128)S(1)}, f32[128]{0:T(128)}, u32[]{:S(2)}) copy-start(f32[128]{0:T(128)} %param.22) | copy-start | bytes 1540
  16.2 3.5 %copy-start.3 = (f32[1,64,128,128]{2,3,1,0:T(8,128)S(1)}, f32[1,64,128,128]{2,3,1,0:T(8,128)}, u32[]{:S(2)}) copy-start(f32[1,64,128,128]{2,3,1,0:T(8,128)} %copy.63) | copy-start | bytes 12582916
  16.3 13.5 %copy-start.2 = (f32[1,16,128,256]{3,2,1,0:T(8,128)S(1)}, f32[1,16,128,256]{3,2,1,0:T(8,128)}, u32[]{:S(2)}) copy-start(f32[1,16,128,256]{3,2,1,0:T(8,128)} %param.19) | copy-start | bytes 6291460
  19.7 11.1 %copy-start.12 = (bf16[256,32]{0,1:T(8,128)(2,1)S(1)}, bf16[256,32]{0,1:T(8,128)(2,1)}, u32[]{:S(2)}) copy-start(bf16[256,32]{0,1:T(8,128)(2,1)} %param.33) | copy-start | bytes 49156
  19.7 11.1 %copy-start.14 = (f32[256]{0:T(256)S(1)}, f32[256]{0:T(256)}, u32[]{:S(2)}) copy-start(f32[256]{0:T(256)} %param.24) | copy-start | bytes 3076
  29.7 71.7 %all-gather.11.cloned.1.call-start = ((), (), s32[]{:S(2)}) async-start(), calls=%async_computation.4 | async-start | bytes 3145728 | tf_op jit(solution)/shard_map/all_gather | solution.py:61
  30.1 34.0 %copy-start.16 = (f32[256]{0:T(256)S(1)}, f32[256]{0:T(256)}, u32[]{:S(2)}) copy-start(f32[256]{0:T(256)} %param.21) | copy-start | bytes 3076
  31.8 34.0 %copy-start.8 = (bf16[256,256]{1,0:T(8,128)(2,1)S(1)}, bf16[256,256]{1,0:T(8,128)(2,1)}, u32[]{:S(2)}) copy-start(bf16[256,256]{1,0:T(8,128)(2,1)} %param.28) | copy-start | bytes 393220
  62.4 5.0 %copy-start.9 = (bf16[256,256]{1,0:T(8,128)(2,1)S(1)}, bf16[256,256]{1,0:T(8,128)(2,1)}, u32[]{:S(2)}) copy-start(bf16[256,256]{1,0:T(8,128)(2,1)} %param.29) | copy-start | bytes 393220
  64.0 6.0 %copy-start.13 = (bf16[256,32]{0,1:T(8,128)(2,1)S(1)}, bf16[256,32]{0,1:T(8,128)(2,1)}, u32[]{:S(2)}) copy-start(bf16[256,32]{0,1:T(8,128)(2,1)} %param.34) | copy-start | bytes 49156
  64.0 128.6 %all-gather.7.cloned.1.call-start = ((), (), s32[]{:S(2)}) async-start(), calls=%async_computation.2 | async-start | bytes 3145728 | tf_op jit(solution)/shard_map/all_gather | solution.py:96
  64.8 1.0 copy-start.4
  67.3 19.4 %copy-start.10 = (bf16[256,256]{1,0:T(8,128)(2,1)S(1)}, bf16[256,256]{1,0:T(8,128)(2,1)}, u32[]{:S(2)}) copy-start(bf16[256,256]{1,0:T(8,128)(2,1)} %param.27) | copy-start | bytes 393220
  67.3 141.6 %all-gather.5.cloned.1.call-start = ((), (), s32[]{:S(2)}) async-start(), calls=%async_computation.1 | async-start | bytes 3145728 | tf_op jit(solution)/shard_map/all_gather | solution.py:97
  173.8 3.1 %copy-start.6 = (bf16[512,128]{1,0:T(8,128)(2,1)S(1)}, bf16[512,128]{1,0:T(8,128)(2,1)}, u32[]{:S(2)}) copy-start(bf16[512,128]{1,0:T(8,128)(2,1)} %param.37) | copy-start | bytes 393220
  173.8 3.1 %copy-start.7 = (bf16[128,512]{1,0:T(8,128)(2,1)S(1)}, bf16[128,512]{1,0:T(8,128)(2,1)}, u32[]{:S(2)}) copy-start(bf16[128,512]{1,0:T(8,128)(2,1)} %param.36) | copy-start | bytes 393220
  173.8 3.1 %copy-start.17 = (f32[128]{0:T(128)S(1)}, f32[128]{0:T(128)}, u32[]{:S(2)}) copy-start(f32[128]{0:T(128)} %param.25) | copy-start | bytes 1540
  212.8 8.1 %copy-start.11 = (bf16[256,256]{1,0:T(8,128)(2,1)S(1)}, bf16[256,256]{1,0:T(8,128)(2,1)}, u32[]{:S(2)}) copy-start(bf16[256,256]{1,0:T(8,128)(2,1)} %param.30) | copy-start | bytes 393220
  220.9 2.8 %copy-start.19 = (bf16[1024,256]{1,0:T(8,128)(2,1)S(1)}, bf16[1024,256]{1,0:T(8,128)(2,1)}, u32[]{:S(2)}) copy-start(bf16[1024,256]{1,0:T(8,128)(2,1)} %param.32) | copy-start | bytes 1572868
  220.9 2.8 %copy-start.20 = (f32[256]{0:T(256)S(1)}, f32[256]{0:T(256)}, u32[]{:S(2)}) copy-start(f32[256]{0:T(256)} %param.23) | copy-start | bytes 3076
  221.7 1.4 copy-start.5
  223.7 6.3 %copy-start.1 = (f32[1024,128]{1,0:T(8,128)S(1)}, f32[1024,128]{1,0:T(8,128)}, u32[]{:S(2)}) copy-start(f32[1024,128]{1,0:T(8,128)} %param.35) | copy-start | bytes 1572868
Sparse Core Ops, SparseCore 0:
  29.8 37.7 all-gather.8
  69.2 32.1 all-gather.10
  102.9 33.0 all-gather.6
  137.5 33.0 all-gather.4
